TPU v7x, 32 devices: a whole 2x2x4 slice. The times are simulated.
32 devices in a mesh: row: 4 (over y, core), col: 8 (over z, x).
Axes of the slice: x: 2, y: 2, z: 4, core: 2. Of those that a mesh axis runs over, the one named last changes fastest.
Arguments:
- weight: bfloat16 [8192, 16384], P('row', 'col'), may hold values from -3 to 3
- momentum: float32 [8192, 16384], P('row', 'col'), may hold values from -100 to 100, as said below
- gradient: bfloat16 [8192, 16384], P('row', 'col'), may hold values from -6 to 6
- prev_basis: bfloat16 [16384, 512], P('col'), may hold values from -6 to 6
Outputs:
- new_weight: bfloat16 [8192, 16384], P('row', 'col')
- new_momentum: float32 [8192, 16384], P('row', 'col')
- new_basis: bfloat16 [16384, 512], P('col')
Inputs may be any that keep to these rules, and one draw needn't show every extreme that they name: momentum has rows and columns of different scales.
All inputs are finite; a program needn't handle non-finite values.
Results may differ from a plain program's by a relative error of at most 0.0021.
Values may be sent and summed in bfloat16 or wider, within the bound.
No kernel may reach another device: no remote copies, remote signals or barrier semaphores. Data moves between devices by JAX's collectives and lax.ppermute only.
A program may use at most 128 MiB of HBM per device.

v0:
```python
import jax
import jax.numpy as jnp
from jax import lax
from jax.sharding import PartitionSpec as P

M = 8192
N = 16384
decay_loss = 0.1
step_size = 0.4
epsilon = 1e-06


def orthogonalize(left_factor, gram_matrix):
    lower_tri = jnp.linalg.cholesky(gram_matrix)
    return jax.scipy.linalg.solve_triangular(lower_tri, left_factor.T, lower=True).T


def per_device(weight, momentum, gradient, prev_basis):
    high = lax.Precision.HIGHEST
    buffer = momentum + gradient.astype(jnp.float32)
    partial_left = jnp.dot(buffer, prev_basis.astype(jnp.float32), precision=high)
    left_factor = lax.psum(partial_left, "col")
    gram_matrix = lax.psum(jnp.dot(left_factor.T, left_factor, precision=high), "row")
    orthonormal = orthogonalize(left_factor, gram_matrix)
    right_piece = lax.psum_scatter(
        jnp.dot(buffer.T, orthonormal, precision=high), "row", scatter_dimension=0, tiled=True
    )
    square_sum = lax.psum(jnp.sum(right_piece * right_piece, axis=0), ("row", "col"))
    column_scale = jnp.sqrt(square_sum / N + epsilon)
    basis_piece = (right_piece / column_scale).astype(jnp.bfloat16)
    new_basis = lax.all_gather(basis_piece, "row", axis=0, tiled=True)
    basis_float = new_basis.astype(jnp.float32)
    new_momentum = buffer - decay_loss * jnp.dot(
        orthonormal * column_scale, basis_float.T, precision=high
    )
    update = jnp.dot(orthonormal, basis_float.T, precision=high)
    new_weight = (weight.astype(jnp.float32) - step_size * (M / N) ** 0.5 * update).astype(
        jnp.bfloat16
    )
    return (new_weight, new_momentum, new_basis)


def solution(mesh):
    return jax.shard_map(
        per_device,
        mesh=mesh,
        in_specs=(P("row", "col"), P("row", "col"), P("row", "col"), P("col", None)),
        out_specs=(P("row", "col"), P("row", "col"), P("col", None)),
        check_vma=False,
    )
```

profile of v0, /device:TPU:0, one launch (start us, length us, event | category | flops | bytes accessed | tf_op | source)
XLA Modules:
  0.0 632.8 jit_solution(8107940526218711960)
XLA Ops:
  7.2 1.5 copy-done
  8.8 18.2 %fusion.1 = f32[2048,512]{1,0:T(8,128)} fusion(bf16[2048,512]{1,0:T(8,128)(2,1)S(1)} %copy-done, f32[2048,2048]{1,0:T(8,128)} %param.5, bf16[2048,2048]{1,0:T(8,128)(2,1)} %param.6), kind=kOutput, calls=%fused_computation.6 | convolution fusion | flops 25778192384 | bytes 31457280 | tf_op jit(solution)/shard_map/dot_general | solution.py:21
  27.0 159.2 %all-reduce.4.cloned.1.call-done = f32[2048,512]{1,0:T(8,128)} async-done(((f32[2048,512]{1,0:T(8,128)}), f32[2048,512]{1,0:T(8,128)}) %all-reduce.4.cloned.1.call-update) | async-done | bytes 4194320 | tf_op jit(solution)/shard_map/psum | solution.py:22
  186.2 11.4 %fusion.42 = f32[512,512]{0,1:T(8,128)} fusion(f32[2048,512]{1,0:T(8,128)} %all-reduce.4.cloned.1.call-done), kind=kOutput, calls=%fused_computation.81 | convolution fusion | flops 6442450944 | bytes 5242880 | tf_op jit(solution)/shard_map/dot_general | solution.py:23
  197.9 35.2 %all-reduce.6.cloned.1.call-done = f32[512,512]{0,1:T(8,128)} async-done(((f32[512,512]{0,1:T(8,128)}), f32[512,512]{0,1:T(8,128)}) %all-reduce.6.cloned.1.call-update) | async-done | bytes 1048592 | tf_op jit(solution)/shard_map/psum | solution.py:23
  233.1 1.6 copy.8
  234.7 1.4 fusion.18
  236.1 11.7 %cholesky.104 = f32[128,128]{1,0:T(8,128)S(1)} custom-call(f32[128,128]{1,0:T(8,128)S(1)} %cholesky.266), custom_call_target="Cholesky" | custom-call | tf_op jit(solution)/shard_map/jit(cholesky)/cholesky | solution.py:14
  247.9 9.8 %custom-call.31 = f32[1,128,128]{1,2,0:T(8,128)S(1)} custom-call(f32[1,128,128]{2,1,0:T(8,128)S(1)} %get-tuple-element.30), custom_call_target="InvertDiagBlocksLowerTriangular" | custom-call | tf_op jit(solution)/shard_map/jit(cholesky)/cholesky | solution.py:14
  258.5 11.7 %cholesky.217 = f32[128,128]{1,0:T(8,128)S(1)} custom-call(f32[128,128]{1,0:T(8,128)S(1)} %cholesky.270), custom_call_target="Cholesky" | custom-call | tf_op jit(solution)/shard_map/jit(cholesky)/cholesky | solution.py:14
  270.2 10.2 %custom-call.32 = f32[1,128,128]{1,2,0:T(8,128)S(1)} custom-call(f32[1,128,128]{2,1,0:T(8,128)S(1)} %get-tuple-element.27), custom_call_target="InvertDiagBlocksLowerTriangular" | custom-call | tf_op jit(solution)/shard_map/jit(cholesky)/cholesky | solution.py:14
  281.1 11.7 %cholesky.238 = f32[128,128]{1,0:T(8,128)S(1)} custom-call(f32[128,128]{1,0:T(8,128)S(1)} %cholesky.275), custom_call_target="Cholesky" | custom-call | tf_op jit(solution)/shard_map/jit(cholesky)/cholesky | solution.py:14
  293.5 9.8 %custom-call.33 = f32[1,128,128]{1,2,0:T(8,128)S(1)} custom-call(f32[1,128,128]{2,1,0:T(8,128)S(1)} %get-tuple-element.24), custom_call_target="InvertDiagBlocksLowerTriangular" | custom-call | tf_op jit(solution)/shard_map/jit(cholesky)/cholesky | solution.py:14
  303.9 11.7 %cholesky.255 = f32[128,128]{1,0:T(8,128)S(1)} custom-call(f32[128,128]{1,0:T(8,128)S(1)} %convolution_subtract_fusion.4), custom_call_target="Cholesky" | custom-call | tf_op jit(solution)/shard_map/jit(cholesky)/cholesky | solution.py:14
  319.8 8.0 %while.1 = (s32[]{:T(128)}, f32[512,512]{1,0:T(8,128)S(1)}, s32[4,2]{0,1:T(2,128)S(1)}, f32[4,128,128]{2,1,0:T(8,128)S(1)}, s32[]{:T(128)}) while((s32[]{:T(128)}, f32[512,512]{1,0:T(8,128)S(1)}, s32[4,2]{0,1:T(2,128)S(1)}, f32[4,128,128]{2,1,0:T(8,128)S(1)}, s32[]{:T(128)}) %tuple.31), condition=%wide.while_cond, body=%wide.while_body.sunk | while | flops 2 | bytes 131181 | solution.py:15
  320.4 1.4 bitcast_dynamic-update-slice_fusion.2
  322.4 1.4 bitcast_dynamic-update-slice_fusion.2
  324.4 1.4 bitcast_dynamic-update-slice_fusion.2
  326.4 1.4 bitcast_dynamic-update-slice_fusion.2
  327.9 39.3 %custom-call.34 = f32[4,128,128]{1,2,0:T(8,128)S(1)} custom-call(f32[4,128,128]{2,1,0:T(8,128)S(1)} %get-tuple-element.10), custom_call_target="InvertDiagBlocksLowerTriangular" | custom-call | tf_op jit(solution)/shard_map/jit(_solve_triangular)/triangular_solve | solution.py:15
  367.2 2.4 fusion.16
  369.6 3.1 convolution_subtract_fusion.1
  373.8 5.0 convolution_subtract_fusion
  379.9 7.2 %fusion.9 = f32[128,2048]{0,1:T(8,128)S(1)} fusion(f32[128,2048]{1,0:T(8,128)S(1)} %fusion.28, f32[128,2048]{1,0:T(8,128)S(1)} %fusion.30, f32[128,2048]{1,0:T(8,128)S(1)} %fusion.16, f32[512,2048]{0,1:T(8,128)S(1)} %bitcast.57, f32[512,512]{1,0:T(8,128)} %copy-done.7), kind=kOutput, calls=%fused_computation.15 | convolution fusion | flops 1209794560 | bytes 5439488 | tf_op jit(solution)/shard_map/jit(_solve_triangular)/triangular_solve | solution.py:15
  389.2 56.3 %fusion = f32[2048,512]{1,0:T(8,128)} fusion(f32[2048,2048]{1,0:T(8,128)} %param.5, bf16[2048,2048]{1,0:T(8,128)(2,1)S(1)} %bitcast.59, f32[128,2048]{1,0:T(8,128)S(1)} %fusion.27, f32[128,2048]{1,0:T(8,128)S(1)} %fusion.28, f32[128,2048]{1,0:T(8,128)S(1)} %fusion.30, f32[128,2048]{1,0:T(8,128)S(1)} %fusion.16), kind=kOutput, calls=%fused_computation.5 | convolution fusion | flops 25781338112 | bytes 33554432 | tf_op jit(solution)/shard_map/dot_general | solution.py:26
  445.6 45.2 %reduce-scatter.2.cloned.1.call-done = f32[512,512]{1,0:T(8,128)} async-done(((f32[2048,512]{1,0:T(8,128)}), f32[512,512]{1,0:T(8,128)}) %reduce-scatter.2.cloned.1.call-update) | async-done | bytes 1048592 | tf_op jit(solution)/shard_map/reduce_scatter | solution.py:25
  490.8 1.3 multiply_reduce_fusion
  492.1 39.3 %psum.23 = f32[512]{0:T(512)S(1)} all-reduce(f32[512]{0:T(512)S(1)} %multiply_reduce_fusion), channel_id=1, replica_groups=mesh['row'=4,'col'=8] {'row','col'}, use_global_device_ids=true, to_apply=%region_12.13 | all-reduce | flops 512 | bytes 4096 | tf_op jit(solution)/shard_map/psum | solution.py:28
  531.4 2.1 divide_convert_fusion
  533.6 23.5 %all-gather.2.cloned.1.call-done = bf16[2048,512]{1,0:T(8,128)(2,1)} async-done(((bf16[512,512]{1,0:T(8,128)(2,1)}), bf16[2048,512]{1,0:T(8,128)(2,1)}) %all-gather.2.cloned.1.call-update) | async-done | bytes 2097168 | tf_op jit(solution)/shard_map/all_gather | solution.py:31
  557.1 35.6 %multiply_subtract_fusion = f32[2048,2048]{1,0:T(8,128)} fusion(bf16[2048,512]{1,0:T(8,128)(2,1)} %all-gather.2.cloned.1.call-done, f32[2048,2048]{1,0:T(8,128)} %param.5, bf16[2048,2048]{1,0:T(8,128)(2,1)} %param.6, f32[512]{0:T(512)S(1)} %add_sqrt_fusion, f32[128,2048]{1,0:T(8,128)} %copy-done.6, f32[128,2048]{1,0:T(8,128)S(1)} %fusion.28, ...), kind=kOutput, calls=%fused_computation.2 | convolution fusion | flops 25790775296 | bytes 48236544 | tf_op jit(solution)/shard_map/dot_general | solution.py:33
  592.7 32.0 %subtract_convert_fusion = bf16[2048,2048]{1,0:T(8,128)(2,1)} fusion(bf16[2048,2048]{1,0:T(8,128)(2,1)} %param.4, bf16[2048,512]{1,0:T(8,128)(2,1)} %all-gather.2.cloned.1.call-done, f32[128,2048]{1,0:T(8,128)} %copy-done.6, f32[128,2048]{1,0:T(8,128)} %copy-done.4, f32[128,2048]{1,0:T(8,128)} %copy-done.3, f32[128,2048]{1,0:T(8,128)S(1)} %fusion.16), kind=kOutput, calls=%fused_computation.3 | convolution fusion | flops 25789726720 | bytes 23068672 | tf_op jit(solution)/shard_map/dot_general | solution.py:36
  (62 shorter events, 12.8 us)
Async XLA Ops:
  7.2 1.6 copy-start
  7.2 179.1 %all-reduce.4.cloned.1.call-start = ((), (), s32[]{:S(2)}) async-start(), calls=%async_computation.1 | async-start | bytes 8388608 | tf_op jit(solution)/shard_map/psum | solution.py:22
  27.0 206.1 %all-reduce.6.cloned.1.call-start = ((), (), s32[]{:S(2)}) async-start(), calls=%async_computation.2 | async-start | bytes 2097152 | tf_op jit(solution)/shard_map/psum | solution.py:23
  197.7 293.1 %reduce-scatter.2.cloned.1.call-start = ((), (), s32[]{:S(2)}) async-start(), calls=%async_computation.3 | async-start | bytes 5242880 | tf_op jit(solution)/shard_map/reduce_scatter | solution.py:25
  327.8 39.3 %copy-start.7 = (f32[512,512]{1,0:T(8,128)}, f32[512,512]{1,0:T(8,128)S(1)}, u32[]{:S(2)}) copy-start(f32[512,512]{1,0:T(8,128)S(1)} %get-tuple-element.99) | copy-start | bytes 3145732
  367.2 6.6 %copy-start.2 = (f32[2048,512]{1,0:T(8,128)S(1)}, f32[2048,512]{1,0:T(8,128)}, u32[]{:S(2)}) copy-start(f32[2048,512]{1,0:T(8,128)} %all-reduce.4.cloned.1.call-done) | copy-start | bytes 12582916
  372.7 16.5 %slice-start = ((s8[8388608]{0:T(1024)(128)(4,1)}), s8[4194304]{0:T(1024)(128)(4,1)S(1)}, s32[]{:S(2)}) async-start(s8[8388608]{0:T(1024)(128)(4,1)} %bitcast.58), calls=%async_computation.5 | async-start | bytes 8388608
  373.8 183.2 %copy-start.3 = (f32[128,2048]{1,0:T(8,128)}, f32[128,2048]{1,0:T(8,128)S(1)}, u32[]{:S(2)}) copy-start(f32[128,2048]{1,0:T(8,128)S(1)} %fusion.30) | copy-start | bytes 3145732
  378.8 10.4 %slice-start.1 = ((s8[8388608]{0:T(1024)(128)(4,1)}), s8[4194304]{0:T(1024)(128)(4,1)S(1)}, s32[]{:S(2)}) async-start(s8[8388608]{0:T(1024)(128)(4,1)} %bitcast.58), calls=%async_computation.6 | async-start | bytes 8388608
  379.9 177.2 %copy-start.4 = (f32[128,2048]{1,0:T(8,128)}, f32[128,2048]{1,0:T(8,128)S(1)}, u32[]{:S(2)}) copy-start(f32[128,2048]{1,0:T(8,128)S(1)} %fusion.28) | copy-start | bytes 3145732
  388.2 1.0 copy-start.6
  445.6 111.5 %all-gather.2.cloned.1.call-start = ((), (), s32[]{:S(2)}) async-start(), calls=%async_computation.4 | async-start | bytes 2621440 | tf_op jit(solution)/shard_map/all_gather | solution.py:31
  592.7 32.1 %copy-start.5 = (bf16[2048,512]{1,0:T(8,128)(2,1)S(1)}, bf16[2048,512]{1,0:T(8,128)(2,1)}, u32[]{:S(2)}) copy-start(bf16[2048,512]{1,0:T(8,128)(2,1)} %all-gather.2.cloned.1.call-done) | copy-start | bytes 6291460
  592.7 33.4 %copy-start.1 = (bf16[2048,512]{1,0:T(8,128)(2,1)S(1)}, bf16[2048,512]{1,0:T(8,128)(2,1)}, u32[]{:S(2)}) copy-start(bf16[2048,512]{1,0:T(8,128)(2,1)} %param.7) | copy-start | bytes 6291460
Sparse Core Ops, SparseCore 0:
  27.1 159.1 all-reduce.3
  197.8 35.2 all-reduce.5
  445.7 45.0 reduce-scatter.1
  533.7 23.3 all-gather.1
where the time goes:
time: 639 us; the launch traced here: 633 us
  waiting for transfers between devices  263 us (41%)
  matrix products  176 us (28%)
  other arithmetic  123 us (19%)
  blocking collectives  39.3 us (6%)
  between operations  16.8 us (3%)
  local copies, waits for them, and re-layouts  13.5 us (2%)
    psum x1, waiting for transfers between devices, per_device(): left_factor = lax.psum(partial_left, 'col')  159 us
    another operation x14, other arithmetic, orthogonalize(): lower_tri = jnp.linalg.cholesky(gram_matrix)  78.8 us
    dot_general x1, matrix products, per_device(): jnp.dot(buffer.T, orthonormal, precision=high)  56.3 us
    reduce_scatter x1, waiting for transfers between devices, per_device(): lax.psum_scatter(jnp.dot(buffer.T, orthonormal, precision=high), 'row', s...  45.2 us
    another operation x3, other arithmetic, orthogonalize(): jax.scipy.linalg.solve_triangular(lower_tri, left_factor.T, lower=True)  39.6 us
    psum x1, blocking collectives, per_device(): lax.psum(jnp.sum(right_piece * right_piece, axis=0), ('row', 'col'))  39.3 us
    dot_general x1, matrix products, per_device(): jnp.dot(orthonormal * column_scale, basis_float.T, precision=high)  35.6 us
    psum x1, waiting for transfers between devices, per_device(): lax.psum(jnp.dot(left_factor.T, left_factor, precision=high), 'row')  35.2 us
  transfers between devices with their start and end apart: 4, of which 4 were waited for; matrix products, arithmetic and copies ran while one was open for 0% of the time, Pallas kernels for 0%

commit v1 on v0

--- a/solution.py
+++ b/solution.py
@@ -8,6 +8,25 @@
 decay_loss = 0.1
 step_size = 0.4
 epsilon = 1e-06
+
+
+def joined_along(blocks, dim):
+    blocks = jnp.moveaxis(blocks, 0, dim)
+    shape = blocks.shape
+    return blocks.reshape(*shape[:dim], shape[dim] * shape[dim + 1], *shape[dim + 2 :])
+
+
+def collected_by_bits(x, axis):
+    length, position = (lax.axis_size(axis), lax.axis_index(axis))
+    parts, apart = (x[None], 1)
+    while apart < length:
+        partner_block = lax.ppermute(parts, axis, [(i, i ^ apart) for i in range(length)])
+        low = position & apart == 0
+        parts = jnp.concatenate(
+            [jnp.where(low, parts, partner_block), jnp.where(low, partner_block, parts)]
+        )
+        apart *= 2
+    return parts
 
 
 def orthogonalize(left_factor, gram_matrix):
@@ -28,7 +47,7 @@
     square_sum = lax.psum(jnp.sum(right_piece * right_piece, axis=0), ("row", "col"))
     column_scale = jnp.sqrt(square_sum / N + epsilon)
     basis_piece = (right_piece / column_scale).astype(jnp.bfloat16)
-    new_basis = lax.all_gather(basis_piece, "row", axis=0, tiled=True)
+    new_basis = joined_along(collected_by_bits(basis_piece, "row"), 0)
     basis_float = new_basis.astype(jnp.float32)
     new_momentum = buffer - decay_loss * jnp.dot(
         orthonormal * column_scale, basis_float.T, precision=high

time: 639 us -> 649 us (1.016)
    ppermute x0 -> x2, waiting for transfers between devices: none -> 26 us  [collected_by_bits(): lax.ppermute(parts, axis, [(i, i ^ apart) for i in range(length)])]
    all_gather x1 -> x0, waiting for transfers between devices: 23.5 us -> none  [per_device(): new_basis = lax.all_gather(basis_piece, 'row', axis=0, tiled=True)]
  transfers between devices with their start and end apart: 4 -> 5, of which waited for: 4 -> 5; matrix products, arithmetic and copies ran while one was open for 0% -> 0% of each run, Pallas kernels for 0% -> 0%
where the time goes in v1:
time: 649 us; the launch traced here: 643 us
  waiting for transfers between devices  266 us (41%)
  matrix products  176 us (27%)
  other arithmetic  129 us (20%)
  blocking collectives  39.3 us (6%)
  between operations  16.8 us (3%)
  local copies, waits for them, and re-layouts  13 us (2%)
    psum x1, waiting for transfers between devices, per_device(): left_factor = lax.psum(partial_left, 'col')  159 us
    another operation x14, other arithmetic, orthogonalize(): lower_tri = jnp.linalg.cholesky(gram_matrix)  78.8 us
    dot_general x1, matrix products, per_device(): jnp.dot(buffer.T, orthonormal, precision=high)  56.7 us
    reduce_scatter x1, waiting for transfers between devices, per_device(): lax.psum_scatter(jnp.dot(buffer.T, orthonormal, precision=high), 'row', s...  45.2 us
    another operation x3, other arithmetic, orthogonalize(): jax.scipy.linalg.solve_triangular(lower_tri, left_factor.T, lower=True)  39.6 us
    psum x1, blocking collectives, per_device(): lax.psum(jnp.sum(right_piece * right_piece, axis=0), ('row', 'col'))  39.3 us
    dot_general x1, matrix products, per_device(): jnp.dot(orthonormal * column_scale, basis_float.T, precision=high)  35.6 us
    psum x1, waiting for transfers between devices, per_device(): lax.psum(jnp.dot(left_factor.T, left_factor, precision=high), 'row')  35.2 us
  transfers between devices with their start and end apart: 5, of which 5 were waited for; matrix products, arithmetic and copies ran while one was open for 0% of the time, Pallas kernels for 0%

profile of v1, /device:TPU:0, one launch (start us, length us, event | category | flops | bytes accessed | tf_op | source)
XLA Modules:
  0.0 642.8 jit_solution(13984277197844494503)
XLA Ops:
  7.2 1.5 copy-done
  8.8 18.2 %fusion.1 = f32[2048,512]{1,0:T(8,128)} fusion(bf16[2048,512]{1,0:T(8,128)(2,1)S(1)} %copy-done, f32[2048,2048]{1,0:T(8,128)} %param.5, bf16[2048,2048]{1,0:T(8,128)(2,1)} %param.6), kind=kOutput, calls=%fused_computation.6 | convolution fusion | flops 25778192384 | bytes 31457280 | tf_op jit(solution)/shard_map/dot_general | solution.py:40
  27.0 159.2 %all-reduce.4.cloned.1.call-done = f32[2048,512]{1,0:T(8,128)} async-done(((f32[2048,512]{1,0:T(8,128)}), f32[2048,512]{1,0:T(8,128)}) %all-reduce.4.cloned.1.call-update) | async-done | bytes 4194320 | tf_op jit(solution)/shard_map/psum | solution.py:41
  186.2 11.4 %fusion.43 = f32[512,512]{0,1:T(8,128)} fusion(f32[2048,512]{1,0:T(8,128)} %all-reduce.4.cloned.1.call-done), kind=kOutput, calls=%fused_computation.88 | convolution fusion | flops 6442450944 | bytes 5242880 | tf_op jit(solution)/shard_map/dot_general | solution.py:42
  197.9 35.2 %all-reduce.6.cloned.1.call-done = f32[512,512]{0,1:T(8,128)} async-done(((f32[512,512]{0,1:T(8,128)}), f32[512,512]{0,1:T(8,128)}) %all-reduce.6.cloned.1.call-update) | async-done | bytes 1048592 | tf_op jit(solution)/shard_map/psum | solution.py:42
  233.1 1.6 copy.8
  234.7 1.4 fusion.18
  236.1 11.7 %cholesky.104 = f32[128,128]{1,0:T(8,128)S(1)} custom-call(f32[128,128]{1,0:T(8,128)S(1)} %cholesky.266), custom_call_target="Cholesky" | custom-call | tf_op jit(solution)/shard_map/jit(cholesky)/cholesky | solution.py:33
  247.9 9.8 %custom-call.31 = f32[1,128,128]{1,2,0:T(8,128)S(1)} custom-call(f32[1,128,128]{2,1,0:T(8,128)S(1)} %get-tuple-element.34), custom_call_target="InvertDiagBlocksLowerTriangular" | custom-call | tf_op jit(solution)/shard_map/jit(cholesky)/cholesky | solution.py:33
  258.5 11.7 %cholesky.217 = f32[128,128]{1,0:T(8,128)S(1)} custom-call(f32[128,128]{1,0:T(8,128)S(1)} %cholesky.270), custom_call_target="Cholesky" | custom-call | tf_op jit(solution)/shard_map/jit(cholesky)/cholesky | solution.py:33
  270.2 10.2 %custom-call.32 = f32[1,128,128]{1,2,0:T(8,128)S(1)} custom-call(f32[1,128,128]{2,1,0:T(8,128)S(1)} %get-tuple-element.31), custom_call_target="InvertDiagBlocksLowerTriangular" | custom-call | tf_op jit(solution)/shard_map/jit(cholesky)/cholesky | solution.py:33
  281.1 11.7 %cholesky.238 = f32[128,128]{1,0:T(8,128)S(1)} custom-call(f32[128,128]{1,0:T(8,128)S(1)} %cholesky.275), custom_call_target="Cholesky" | custom-call | tf_op jit(solution)/shard_map/jit(cholesky)/cholesky | solution.py:33
  293.5 9.8 %custom-call.33 = f32[1,128,128]{1,2,0:T(8,128)S(1)} custom-call(f32[1,128,128]{2,1,0:T(8,128)S(1)} %get-tuple-element.28), custom_call_target="InvertDiagBlocksLowerTriangular" | custom-call | tf_op jit(solution)/shard_map/jit(cholesky)/cholesky | solution.py:33
  303.9 11.7 %cholesky.255 = f32[128,128]{1,0:T(8,128)S(1)} custom-call(f32[128,128]{1,0:T(8,128)S(1)} %convolution_subtract_fusion.4), custom_call_target="Cholesky" | custom-call | tf_op jit(solution)/shard_map/jit(cholesky)/cholesky | solution.py:33
  319.8 8.0 %while.1 = (s32[]{:T(128)}, f32[512,512]{1,0:T(8,128)S(1)}, s32[4,2]{0,1:T(2,128)S(1)}, f32[4,128,128]{2,1,0:T(8,128)S(1)}, s32[]{:T(128)}) while((s32[]{:T(128)}, f32[512,512]{1,0:T(8,128)S(1)}, s32[4,2]{0,1:T(2,128)S(1)}, f32[4,128,128]{2,1,0:T(8,128)S(1)}, s32[]{:T(128)}) %tuple.33), condition=%wide.while_cond, body=%wide.while_body.sunk | while | flops 2 | bytes 131181 | solution.py:34
  327.9 39.3 %custom-call.34 = f32[4,128,128]{1,2,0:T(8,128)S(1)} custom-call(f32[4,128,128]{2,1,0:T(8,128)S(1)} %get-tuple-element.10), custom_call_target="InvertDiagBlocksLowerTriangular" | custom-call | tf_op jit(solution)/shard_map/jit(_solve_triangular)/triangular_solve | solution.py:34
  367.2 2.4 fusion.16
  369.6 3.1 convolution_subtract_fusion.1
  373.8 5.0 convolution_subtract_fusion
  379.9 6.8 %fusion.9 = f32[128,2048]{0,1:T(8,128)S(1)} fusion(f32[128,2048]{1,0:T(8,128)S(1)} %fusion.29, f32[128,2048]{1,0:T(8,128)S(1)} %fusion.31, f32[128,2048]{1,0:T(8,128)S(1)} %fusion.16, f32[512,2048]{0,1:T(8,128)S(1)} %bitcast.62, f32[512,512]{1,0:T(8,128)} %copy-done.8), kind=kOutput, calls=%fused_computation.15 | convolution fusion | flops 1209794560 | bytes 5439488 | tf_op jit(solution)/shard_map/jit(_solve_triangular)/triangular_solve | solution.py:34
  388.8 56.7 %fusion = f32[2048,512]{1,0:T(8,128)} fusion(f32[2048,2048]{1,0:T(8,128)} %param.5, bf16[2048,2048]{1,0:T(8,128)(2,1)S(1)} %bitcast.64, f32[128,2048]{1,0:T(8,128)S(1)} %fusion.28, f32[128,2048]{1,0:T(8,128)S(1)} %fusion.29, f32[128,2048]{1,0:T(8,128)S(1)} %fusion.31, f32[128,2048]{1,0:T(8,128)S(1)} %fusion.16), kind=kOutput, calls=%fused_computation.5 | convolution fusion | flops 25781338112 | bytes 33554432 | tf_op jit(solution)/shard_map/dot_general | solution.py:45
  445.6 45.2 %reduce-scatter.2.cloned.1.call-done = f32[512,512]{1,0:T(8,128)} async-done(((f32[2048,512]{1,0:T(8,128)}), f32[512,512]{1,0:T(8,128)}) %reduce-scatter.2.cloned.1.call-update) | async-done | bytes 1048592 | tf_op jit(solution)/shard_map/reduce_scatter | solution.py:44
  492.1 39.3 %psum.23 = f32[512]{0:T(512)S(1)} all-reduce(f32[512]{0:T(512)S(1)} %multiply_reduce_fusion), channel_id=1, replica_groups=mesh['row'=4,'col'=8] {'row','col'}, use_global_device_ids=true, to_apply=%region_12.13 | all-reduce | flops 512 | bytes 4096 | tf_op jit(solution)/shard_map/psum | solution.py:47
  531.4 2.1 fusion.19
  533.6 2.2 collective-permute-done
  535.8 1.5 broadcast_select_fusion.3
  539.2 2.3 collective-permute-start.1
  541.4 23.8 %collective-permute-done.1 = bf16[2,512,512]{2,1,0:T(8,128)(2,1)} collective-permute-done((bf16[2,512,512]{2,1,0:T(8,128)(2,1)}, bf16[2,512,512]{2,1,0:T(8,128)(2,1)}, u32[]{:S(2)}, u32[]{:S(2)}) %collective-permute-start.1) | collective-permute-done | bytes 1048608 | tf_op jit(solution)/shard_map/ppermute | solution.py:23
  565.2 1.7 broadcast_select_fusion.1
  566.9 1.5 pad_maximum_fusion.1
  568.4 35.6 %multiply_subtract_fusion = f32[2048,2048]{1,0:T(8,128)} fusion(bf16[2048,512]{1,0:T(8,128)(2,1)} %bitcast.65, f32[2048,2048]{1,0:T(8,128)} %param.5, bf16[2048,2048]{1,0:T(8,128)(2,1)} %param.6, f32[512]{0:T(512)S(1)} %add_sqrt_fusion, f32[128,2048]{1,0:T(8,128)} %copy-done.7, f32[128,2048]{1,0:T(8,128)S(1)} %fusion.29, f32[128,2048]{1,0:T(8,128)S(1)} %fusion.31, ...), kind=kOutput, calls=%fused_computation.2 | convolution fusion | flops 25790775296 | bytes 48236544 | tf_op jit(solution)/shard_map/dot_general | solution.py:52
  604.0 32.0 %subtract_convert_fusion = bf16[2048,2048]{1,0:T(8,128)(2,1)} fusion(bf16[2048,2048]{1,0:T(8,128)(2,1)} %param.4, bf16[2048,512]{1,0:T(8,128)(2,1)} %bitcast.66, f32[128,2048]{1,0:T(8,128)} %copy-done.7, f32[128,2048]{1,0:T(8,128)} %copy-done.4, f32[128,2048]{1,0:T(8,128)} %copy-done.3, f32[128,2048]{1,0:T(8,128)S(1)} %fusion.16), kind=kOutput, calls=%fused_computation.3 | convolution fusion | flops 25789726720 | bytes 23068672 | tf_op jit(solution)/shard_map/dot_general | solution.py:55
  (68 shorter events, 20.2 us)
Async XLA Ops:
  7.2 1.6 copy-start
  7.2 179.1 %all-reduce.4.cloned.1.call-start = ((), (), s32[]{:S(2)}) async-start(), calls=%async_computation.1 | async-start | bytes 8388608 | tf_op jit(solution)/shard_map/psum | solution.py:41
  27.0 206.1 %all-reduce.6.cloned.1.call-start = ((), (), s32[]{:S(2)}) async-start(), calls=%async_computation.2 | async-start | bytes 2097152 | tf_op jit(solution)/shard_map/psum | solution.py:42
  197.7 293.1 %reduce-scatter.2.cloned.1.call-start = ((), (), s32[]{:S(2)}) async-start(), calls=%async_computation.3 | async-start | bytes 5242880 | tf_op jit(solution)/shard_map/reduce_scatter | solution.py:44
  327.8 39.3 %copy-start.8 = (f32[512,512]{1,0:T(8,128)}, f32[512,512]{1,0:T(8,128)S(1)}, u32[]{:S(2)}) copy-start(f32[512,512]{1,0:T(8,128)S(1)} %get-tuple-element.95) | copy-start | bytes 3145732
  367.2 6.6 %copy-start.2 = (f32[2048,512]{1,0:T(8,128)S(1)}, f32[2048,512]{1,0:T(8,128)}, u32[]{:S(2)}) copy-start(f32[2048,512]{1,0:T(8,128)} %all-reduce.4.cloned.1.call-done) | copy-start | bytes 12582916
  372.7 16.1 %slice-start = ((s8[8388608]{0:T(1024)(128)(4,1)}), s8[4194304]{0:T(1024)(128)(4,1)S(1)}, s32[]{:S(2)}) async-start(s8[8388608]{0:T(1024)(128)(4,1)} %bitcast.63), calls=%async_computation.4 | async-start | bytes 8388608
  373.8 194.6 %copy-start.3 = (f32[128,2048]{1,0:T(8,128)}, f32[128,2048]{1,0:T(8,128)S(1)}, u32[]{:S(2)}) copy-start(f32[128,2048]{1,0:T(8,128)S(1)} %fusion.31) | copy-start | bytes 3145732
  378.8 10.0 %slice-start.1 = ((s8[8388608]{0:T(1024)(128)(4,1)}), s8[4194304]{0:T(1024)(128)(4,1)S(1)}, s32[]{:S(2)}) async-start(s8[8388608]{0:T(1024)(128)(4,1)} %bitcast.63), calls=%async_computation.5 | async-start | bytes 8388608
  379.9 188.5 %copy-start.4 = (f32[128,2048]{1,0:T(8,128)}, f32[128,2048]{1,0:T(8,128)S(1)}, u32[]{:S(2)}) copy-start(f32[128,2048]{1,0:T(8,128)S(1)} %fusion.29) | copy-start | bytes 3145732
  387.8 1.0 copy-start.7
  533.6 2.3 collective-permute-start
  537.3 0.8 copy-start.5
  537.3 1.8 copy-start.6
  539.2 26.0 %collective-permute-start.1 = (bf16[2,512,512]{2,1,0:T(8,128)(2,1)}, bf16[2,512,512]{2,1,0:T(8,128)(2,1)}, u32[]{:S(2)}, u32[]{:S(2)}) collective-permute-start(bf16[2,512,512]{2,1,0:T(8,128)(2,1)} %pad_maximum_fusion.2), channel_id=1, source_target_pairs={{0,16},{8,24},{16,0},{24,8},{1,17},{9,25},{17,1},{25,9},{2,18},{10... | collective-permute-start | bytes 3145736 | tf_op jit(solution)/shard_map/ppermute | solution.py:23
  604.0 32.0 %copy-start.1 = (bf16[2048,512]{1,0:T(8,128)(2,1)S(1)}, bf16[2048,512]{1,0:T(8,128)(2,1)}, u32[]{:S(2)}) copy-start(bf16[2048,512]{1,0:T(8,128)(2,1)} %param.7) | copy-start | bytes 6291460
Sparse Core Ops, SparseCore 0:
  27.1 159.1 all-reduce.3
  197.8 35.2 all-reduce.5
  445.7 45.0 reduce-scatter.1
